TPU v7x, 128 devices: a whole 4x4x4 slice. The times are simulated.
128 devices in a mesh: dp: 4 (over x), expert: 32 (over y, z, core).
Axes of the slice: x: 4, y: 4, z: 4, core: 2. Of those that a mesh axis runs over, the one named last changes fastest.
Arguments:
- tokens: bfloat16 [4096, 3584], P(('dp', 'expert')), may hold values from -6 to 6
- expert_ids: int32 [4096, 8], P(('dp', 'expert')), may hold values from 0 to 31, all different within a row; in each aligned block of 32 rows (0 to 31, 32 to 63, ...) at most 12 rows name the same one
- route_weights: float32 [4096, 8], P(('dp', 'expert')), may hold values from 0.1 to 1
- out_grad: bfloat16 [4096, 3584], P(('dp', 'expert')), may hold values from -6 to 6
- gate_weight: bfloat16 [32, 3584, 1024], P('expert', 'dp'), may hold values from -0.09375 to 0.09375
- up_weight: bfloat16 [32, 3584, 1024], P('expert', 'dp'), may hold values from -0.09375 to 0.09375
- down_weight: bfloat16 [32, 1024, 3584], P('expert', None, 'dp'), may hold values from -0.1875 to 0.1875
Outputs:
- mixed: bfloat16 [4096, 3584], P(('dp', 'expert'))
- tokens_grad: bfloat16 [4096, 3584], P(('dp', 'expert'))
- route_grad: float32 [4096, 8], P(('dp', 'expert'))
- gate_grad: bfloat16 [32, 3584, 1024], P('expert', 'dp')
- up_grad: bfloat16 [32, 3584, 1024], P('expert', 'dp')
- down_grad: bfloat16 [32, 1024, 3584], P('expert', None, 'dp')
Inputs may be any that keep to these rules, and one draw needn't show every extreme that they name: `expert_ids`: each row names 8 different experts; in each aligned block of 32 rows (the rows of one device) no expert is named by more than 12 rows, a bound that some block reaches.
All inputs are finite; a program needn't handle non-finite values.
Results may differ from a plain program's by a relative error of at most 0.0065.
Values may be sent and summed in bfloat16 or wider, within the bound.
A program may use at most 192 MiB of HBM per device.

v0:
```python
import jax
import jax.numpy as jnp
from jax import lax
from jax.sharding import PartitionSpec as P

BF = jnp.bfloat16
F32 = jnp.float32
LANES = 128


def dot32(a, b, dims):
    return lax.dot_general(a, b, (dims, ((), ())), preferred_element_type=F32)


def route_table(ids, weights, experts):
    onehot = (ids[:, :, None] == jnp.arange(experts, dtype=jnp.int32)).astype(jnp.int32)
    chosen = jnp.sum(onehot, axis=1)
    place = jnp.cumsum(chosen, axis=0) * chosen
    dense = jnp.sum(onehot.astype(F32) * weights[:, :, None], axis=1)
    high = lax.reduce_precision(dense, 8, 7)
    middle = lax.reduce_precision(dense - high, 8, 7)
    low = dense - high - middle
    return jnp.concatenate([place.astype(F32), high, middle, low], axis=1).astype(BF)


def to_slices(array, n_dp):
    rows, width = array.shape
    return lax.all_to_all(array, "dp", split_axis=1, concat_axis=0, tiled=True)


def dispatch(tokens, out_grad, table):
    n_dp = lax.axis_size("dp")
    tok = to_slices(tokens, n_dp)
    grad = to_slices(out_grad, n_dp)
    tab = lax.all_gather(table, "dp", axis=0, tiled=True)
    whole = lax.all_gather(jnp.concatenate([tok, grad, tab], axis=1), "expert", axis=0, tiled=False)
    return (whole, grad, tab)


def pick_rows(whole, slots, experts, n_dp, tok_rows, width):
    me = lax.axis_index("expert")
    tab = whole[:, :, 2 * width :].astype(F32)
    lane = jnp.arange(tab.shape[2], dtype=jnp.int32)
    place = jnp.sum(jnp.where(lane == me, tab, 0.0), axis=2)
    weight = jnp.sum(jnp.where((lane >= experts) & (lane % experts == me), tab, 0.0), axis=2)
    rows = n_dp * slots
    row = jnp.arange(rows, dtype=jnp.int32)
    tok = jnp.arange(n_dp * tok_rows, dtype=jnp.int32)
    same = row[:, None] // slots == tok[None, :] // tok_rows
    hit = same & (place[:, None, :] == (row % slots + 1).astype(F32)[None, :, None])
    picked = lax.dot_general(
        hit.astype(BF),
        whole[:, :, : 2 * width],
        (((2,), (1,)), ((0,), (0,))),
        preferred_element_type=F32,
    )
    scale = jnp.sum(jnp.where(hit, weight[:, None, :], 0.0), axis=2)
    x_rows = picked[:, :, :width].astype(BF).reshape(experts * rows, width)
    g_rows = (picked[:, :, width:] * scale[:, :, None]).astype(BF).reshape(experts * rows, width)
    return (x_rows, g_rows)


def activations(pre, quarter):
    gate, up, hgrad = (pre[:, i * quarter : (i + 1) * quarter].astype(F32) for i in range(3))
    sig = jax.nn.sigmoid(gate)
    act = gate * sig
    slope = sig * (1.0 + gate * (1.0 - sig))
    return jnp.concatenate(
        [(act * up).astype(BF), (hgrad * up * slope).astype(BF), (hgrad * act).astype(BF)], axis=1
    )


def combine(back, ids, grad, tab, slots, experts, n_dp, tok_rows, width):
    tab = tab.astype(F32)
    toks = n_dp * tok_rows
    place = tab[:, :experts]
    weight = (
        tab[:, experts : 2 * experts]
        + tab[:, 2 * experts : 3 * experts]
        + tab[:, 3 * experts : 4 * experts]
    )
    row = jnp.arange(n_dp * slots, dtype=jnp.int32)
    tok = jnp.arange(toks, dtype=jnp.int32)
    same = row[None, :] // slots == tok[:, None] // tok_rows
    hit = same[:, None, :] & (place[:, :, None] == (row % slots + 1).astype(F32))
    flat = hit.reshape(toks, -1)
    scaled = jnp.where(hit, weight[:, :, None], 0.0).reshape(toks, -1)
    out_rows = back[:, :width]
    in_rows = back[:, width:]
    mixed = lax.dot_general(
        scaled, out_rows.astype(F32), (((1,), (0,)), ((), ())), precision=lax.Precision.HIGHEST
    )
    tgrad = dot32(flat.astype(BF), in_rows, ((1,), (0,)))
    dots = dot32(grad, out_rows, ((1,), (1,)))
    route = jnp.sum(jnp.where(hit, dots.reshape(hit.shape), 0.0), axis=2)
    mixed = lax.all_to_all(mixed.astype(BF).reshape(n_dp, tok_rows, width), "dp", 0, 0, tiled=True)
    tgrad = lax.all_to_all(tgrad.astype(BF).reshape(n_dp, tok_rows, width), "dp", 0, 0, tiled=True)
    route = lax.psum_scatter(route, "dp", scatter_dimension=0, tiled=True)
    mixed = mixed.transpose(1, 0, 2).reshape(tok_rows, n_dp * width)
    tgrad = tgrad.transpose(1, 0, 2).reshape(tok_rows, n_dp * width)
    onehot = ids[:, :, None] == jnp.arange(experts, dtype=jnp.int32)
    route = jnp.sum(jnp.where(onehot, route[:, None, :], 0.0), axis=2)
    return (mixed, tgrad, route)


def per_device(tokens, ids, weights, out_grad, gate_weight, up_weight, down_weight):
    experts = lax.axis_size("expert")
    n_dp = lax.axis_size("dp")
    tok_rows, model = tokens.shape
    width = model // n_dp
    hidden = gate_weight.shape[2]
    quarter = hidden // n_dp
    slots = min(tok_rows, 3 * tok_rows * ids.shape[1] // (2 * experts))
    gate, up, down = (gate_weight[0], up_weight[0], down_weight[0])
    table = route_table(ids, weights, experts)
    whole, grad, tab = dispatch(tokens, out_grad, table)
    x_rows, g_rows = pick_rows(whole, slots, experts, n_dp, tok_rows, width)
    rows = x_rows.shape[0]
    part = jnp.stack(
        [
            dot32(x_rows, gate, ((1,), (0,))).astype(BF),
            dot32(x_rows, up, ((1,), (0,))).astype(BF),
            dot32(g_rows, down, ((1,), (1,))).astype(BF),
        ]
    )
    part = (
        part.reshape(3, rows, n_dp, quarter).transpose(2, 1, 0, 3).reshape(n_dp * rows, 3 * quarter)
    )
    pre = lax.psum_scatter(part, "dp", scatter_dimension=0, tiled=True)
    acts = activations(pre, quarter)
    terms = lax.all_gather(acts, "dp", axis=0, tiled=False)
    terms = terms.reshape(n_dp, rows, 3, quarter).transpose(2, 1, 0, 3).reshape(3, rows, hidden)
    hid, gterm, uterm = (terms[0], terms[1], terms[2])
    out_rows = dot32(hid, down, ((1,), (0,))).astype(BF)
    in_rows = (dot32(gterm, gate, ((1,), (1,))) + dot32(uterm, up, ((1,), (1,)))).astype(BF)
    send = jnp.concatenate([out_rows, in_rows], axis=1).reshape(experts, n_dp * slots, 2 * width)
    back = lax.all_to_all(send, "expert", split_axis=0, concat_axis=0, tiled=True)
    back = back.reshape(experts * n_dp * slots, 2 * width)
    gate_grad = dot32(x_rows, gterm, ((0,), (0,))).astype(BF)[None]
    up_grad = dot32(x_rows, uterm, ((0,), (0,))).astype(BF)[None]
    down_grad = dot32(hid, g_rows, ((0,), (0,))).astype(BF)[None]
    mixed, tgrad, route = combine(back, ids, grad, tab, slots, experts, n_dp, tok_rows, width)
    return (mixed, tgrad, route, gate_grad, up_grad, down_grad)


def solution(mesh):
    rows = P(("dp", "expert"), None)
    weights = (P("expert", "dp", None), P("expert", "dp", None), P("expert", None, "dp"))
    return jax.shard_map(
        per_device,
        mesh=mesh,
        in_specs=(rows, rows, rows, rows) + weights,
        out_specs=(rows, rows, rows) + weights,
        check_vma=False,
    )
```

profile of v0, /device:TPU:34, one launch (start us, length us, event | category | flops | bytes accessed | tf_op | source)
XLA Modules:
  0.0 510.5 jit_solution(16522338820058106155)
XLA Ops:
  7.2 1.8 copy.108
  9.0 4.8 all-to-all-start.1
  13.8 0.8 copy.82
  14.7 0.8 copy.83
  15.5 1.6 copy.109
  17.3 1.5 all-to-all-done.1
  18.8 4.8 all-to-all-start
  23.7 11.9 %all_gather.15 = bf16[128,128]{1,0:T(8,128)(2,1)S(1)} all-gather(bf16[32,128]{1,0:T(8,128)(2,1)S(1)} %pad_maximum_fusion.4), channel_id=1, replica_groups=mesh['dp'=4,'expert'=32] {'dp'}, dimensions={0}, use_global_device_ids=true | all-gather | bytes 40960 | tf_op jit(solution)/shard_map/all_gather | solution.py:35
  35.7 0.8 pad_maximum_fusion.3
  36.7 71.4 %all-gather.5.cloned.1.call-done = bf16[4096,1920]{1,0:T(8,128)(2,1)} async-done(((bf16[128,1920]{1,0:T(8,128)(2,1)}), bf16[4096,1920]{1,0:T(8,128)(2,1)}) %all-gather.5.cloned.1.call-update) | async-done | bytes 15728656 | tf_op jit(solution)/shard_map/all_gather | solution.py:36
  108.1 2.0 fusion.10
  110.1 6.4 %fusion = f32[32,48,1792]{2,1,0:T(8,128)S(1)} fusion(bf16[32,128,1920]{2,1,0:T(8,128)(2,1)} %bitcast.95, f32[32,128]{1,0:T(8,128)S(1)} %get-tuple-element.13, f32[48]{0:T(128)S(1)} %fusion.41, pred[48,128]{1,0:T(8,128)(4,1)S(1)} %broadcast_compare_fusion), kind=kOutput, calls=%fused_computation | convolution fusion | flops 705036288 | bytes 25712832 | tf_op jit(solution)/shard_map/dot_general | solution.py:51
  117.6 2.5 copy-done.9
  120.0 3.7 convolution_convert_fusion
  123.7 2.4 copy.90
  126.2 3.8 convolution_convert_fusion.2
  130.0 2.4 copy.88
  132.5 4.3 convolution_convert_fusion.1
  136.8 2.4 copy.89
  139.2 9.2 %pad_maximum_fusion = bf16[3,1536,4,256]{1,2,3,0:T(4,128)(2,1)} fusion(bf16[1,1536,4,256]{1,2,3,0:T(4,128)(2,1)S(1)} %copy.90, bf16[1,1536,4,256]{1,2,3,0:T(4,128)(2,1)S(1)} %copy.89, bf16[1,1536,4,256]{1,2,3,0:T(4,128)(2,1)S(1)} %copy.88), kind=kLoop, calls=%fused_computation.2 | loop fusion | flops 9437184 | bytes 18874368 | tf_op jit(solution)/shard_map/stack | solution.py:119
  148.4 10.3 %copy.105 = bf16[96,8,4,1536]{3,1,2,0:T(8,128)(2,1)} copy(bf16[96,8,4,1536]{3,2,1,0:T(4,128)(2,1)} %bitcast.98) | data formatting | bytes 18874368
  158.8 87.8 %reduce-scatter.5.cloned.1.call-done = bf16[1536,768]{0,1:T(8,128)(2,1)} async-done(((bf16[6144,768]{0,1:T(8,128)(2,1)}), bf16[1536,768]{0,1:T(8,128)(2,1)}) %reduce-scatter.5.cloned.1.call-update) | async-done | bytes 2359312 | tf_op jit(solution)/shard_map/reduce_scatter | solution.py:129
  246.7 2.6 fusion.18
  249.2 1.5 pad_maximum_fusion.2
  250.8 93.0 %all-gather.7.cloned.1.call-done = bf16[6144,768]{0,1:T(8,128)(2,1)} async-done(((bf16[1536,768]{0,1:T(8,128)(2,1)}), bf16[6144,768]{0,1:T(8,128)(2,1)}) %all-gather.7.cloned.1.call-update) | async-done | bytes 9437200 | tf_op jit(solution)/shard_map/all_gather | solution.py:131
  343.8 15.4 %reshape.277 = bf16[4,1536,3,256]{1,0,3,2:T(4,128)(2,1)} reshape(bf16[6144,768]{0,1:T(8,128)(2,1)} %all-gather.7.cloned.1.call-done) | data formatting | bytes 18874368 | tf_op jit(solution)/shard_map/reshape | solution.py:132
  359.3 6.0 %fusion.42 = (bf16[1,1536,4,256]{1,2,3,0:T(4,128)(2,1)S(1)}, bf16[1,1536,4,256]{1,2,3,0:T(4,128)(2,1)S(1)}, bf16[1,1536,4,256]{1,2,3,0:T(4,128)(2,1)S(1)}) fusion(bf16[3,1536,4,256]{1,2,3,0:T(4,128)(2,1)} %bitcast.97), kind=kLoop, calls=%fused_computation.93 | loop fusion | bytes 18874368 | tf_op jit(solution)/shard_map/slice | solution.py:133
  365.9 3.0 fusion.15
  370.1 2.3 copy-done.10
  372.3 3.3 convolution_convert_fusion.3
  375.7 3.3 add_convert_fusion
  379.0 2.8 pad_maximum_fusion.1
  381.8 8.1 %copy.94 = bf16[1536,1792]{1,0:T(8,128)(2,1)} copy(bf16[1536,1792]{0,1:T(8,128)(2,1)} %pad_maximum_fusion.1) | data formatting | bytes 11010048 | tf_op jit(solution)/shard_map/concatenate | solution.py:136
  389.9 7.5 %all-to-all-start.2 = ((bf16[32,48,1792]{2,1,0:T(8,128)(2,1)}), bf16[32,48,1792]{2,1,0:T(8,128)(2,1)}, u32[]{:S(2)}, u32[]{:S(2)}) async-start(bf16[32,48,1792]{2,1,0:T(8,128)(2,1)} %bitcast.99), calls=%async_computation.3 | async-start | bytes 11010048 | tf_op jit(solution)/shard_map/all_to_all | solution.py:137
  398.5 7.5 %convert_bitcast_fusion = bf16[1,1024,896]{2,1,0:T(8,128)(2,1)} fusion(bf16[1536,1024]{0,1:T(8,128)(2,1)} %bitcast.105, bf16[1536,896]{1,0:T(8,128)(2,1)} %bitcast.114), kind=kOutput, calls=%fused_computation.36 | convolution fusion | flops 2819489792 | bytes 7733248 | tf_op jit(solution)/shard_map/dot_general | solution.py:12
  406.0 4.4 convert_bitcast_fusion.1
  410.4 61.9 %all-to-all-done.2 = bf16[32,48,1792]{2,1,0:T(8,128)(2,1)} async-done(((bf16[32,48,1792]{2,1,0:T(8,128)(2,1)}), bf16[32,48,1792]{2,1,0:T(8,128)(2,1)}, u32[]{:S(2)}, u32[]{:S(2)}) %all-to-all-start.2) | async-done | bytes 5505056 | tf_op jit(solution)/shard_map/all_to_all | solution.py:137
  472.3 2.6 fusion.5
  475.2 0.7 copy.99
  476.0 3.1 fusion.30
  479.1 4.5 all-to-all-start.4
  483.6 4.0 fusion.27
  487.6 1.2 all-to-all-done.4
  488.8 4.9 all-to-all-start.3
  493.6 7.1 %convert_bitcast_fusion.2 = bf16[1,896,1024]{2,1,0:T(8,128)(2,1)} fusion(bf16[1536,896]{1,0:T(8,128)(2,1)} %bitcast.111, bf16[1536,1024]{0,1:T(8,128)(2,1)} %bitcast.101), kind=kOutput, calls=%fused_computation.38 | convolution fusion | flops 2819489792 | bytes 7733248 | tf_op jit(solution)/shard_map/dot_general | solution.py:12
  500.8 0.9 select_reduce_fusion.2
  502.3 0.7 copy.104
  503.0 0.7 copy.103
  (64 shorter events, 5.5 us)
Async XLA Ops:
  7.2 119.0 %copy-start = (bf16[1,896,1024]{2,1,0:T(8,128)(2,1)S(1)}, bf16[1,896,1024]{2,1,0:T(8,128)(2,1)}, u32[]{:S(2)}) copy-start(bf16[1,896,1024]{2,1,0:T(8,128)(2,1)} %param.11) | copy-start | bytes 5505028
  9.0 9.9 %all-to-all-start.1 = ((bf16[32,4,896]{2,0,1:T(8,128)(2,1)}), bf16[32,4,896]{2,0,1:T(8,128)(2,1)S(1)}, u32[]{:S(2)}, u32[]{:S(2)}) async-start(bf16[32,4,896]{2,0,1:T(8,128)(2,1)} %bitcast.92), calls=%async_computation.1 | async-start | bytes 458752 | tf_op jit(solution)/shard_map/all_to_all | solution.py:28
  18.8 16.8 %all-to-all-start = ((bf16[32,4,896]{2,0,1:T(8,128)(2,1)}), bf16[32,4,896]{2,0,1:T(8,128)(2,1)S(1)}, u32[]{:S(2)}, u32[]{:S(2)}) async-start(bf16[32,4,896]{2,0,1:T(8,128)(2,1)} %bitcast.93), calls=%async_computation | async-start | bytes 458752 | tf_op jit(solution)/shard_map/all_to_all | solution.py:28
  23.6 84.5 %all-gather.5.cloned.1.call-start = ((), (), s32[]{:S(2)}) async-start(), calls=%async_computation.8 | async-start | bytes 16220160 | tf_op jit(solution)/shard_map/all_gather | solution.py:36
  36.5 210.1 %reduce-scatter.5.cloned.1.call-start = ((), (), s32[]{:S(2)}) async-start(), calls=%async_computation.7 | async-start | bytes 11796480 | tf_op jit(solution)/shard_map/reduce_scatter | solution.py:129
  117.2 15.3 %copy-start.6 = (bf16[32,48,896]{2,1,0:T(8,128)(2,1)}, bf16[32,48,896]{2,1,0:T(8,128)(2,1)S(1)}, u32[]{:S(2)}) copy-start(bf16[32,48,896]{2,1,0:T(8,128)(2,1)S(1)} %slice.117) | copy-start | bytes 8257540
  117.2 2.9 copy-start.9
  117.6 6.2 %copy-start.8 = (bf16[32,48,896]{2,1,0:T(8,128)(2,1)}, bf16[32,48,896]{2,1,0:T(8,128)(2,1)S(1)}, u32[]{:S(2)}) copy-start(bf16[32,48,896]{2,1,0:T(8,128)(2,1)S(1)} %fusion.2) | copy-start | bytes 8257540
  130.0 2.5 copy-start.11
  158.8 185.0 %all-gather.7.cloned.1.call-start = ((), (), s32[]{:S(2)}) async-start(), calls=%async_computation.9 | async-start | bytes 11796480 | tf_op jit(solution)/shard_map/all_gather | solution.py:131
  365.8 3.0 copy-start.2
  369.5 6.3 %copy-start.3 = (bf16[1,1536,4,256]{1,3,2,0:T(8,128)(2,1)}, bf16[1,1536,4,256]{1,3,2,0:T(8,128)(2,1)S(1)}, u32[]{:S(2)}) copy-start(bf16[1,1536,4,256]{1,3,2,0:T(8,128)(2,1)S(1)} %copy.93) | copy-start | bytes 9437188
  369.5 2.9 copy-start.10
  370.1 5.6 %copy-start.5 = (bf16[1,1536,4,256]{1,3,2,0:T(8,128)(2,1)}, bf16[1,1536,4,256]{1,3,2,0:T(8,128)(2,1)S(1)}, u32[]{:S(2)}) copy-start(bf16[1,1536,4,256]{1,3,2,0:T(8,128)(2,1)S(1)} %copy.91) | copy-start | bytes 9437188
  372.3 3.4 copy-start.12
  389.9 82.4 %all-to-all-start.2 = ((bf16[32,48,1792]{2,1,0:T(8,128)(2,1)}), bf16[32,48,1792]{2,1,0:T(8,128)(2,1)}, u32[]{:S(2)}, u32[]{:S(2)}) async-start(bf16[32,48,1792]{2,1,0:T(8,128)(2,1)} %bitcast.99), calls=%async_computation.3 | async-start | bytes 11010048 | tf_op jit(solution)/shard_map/all_to_all | solution.py:137
  397.4 103.3 %reduce-scatter.7.cloned.1.call-start = ((), (), s32[]{:S(2)}) async-start(), calls=%async_computation.10 | async-start | bytes 81920 | tf_op jit(solution)/shard_map/reduce_scatter | solution.py:98
  398.5 7.5 %copy-start.4 = (bf16[1,1536,4,256]{1,3,2,0:T(8,128)(2,1)S(1)}, bf16[1,1536,4,256]{1,3,2,0:T(8,128)(2,1)}, u32[]{:S(2)}) copy-start(bf16[1,1536,4,256]{1,3,2,0:T(8,128)(2,1)} %copy-done.3) | copy-start | bytes 9437188
  398.5 7.5 %copy-start.7 = (bf16[32,48,896]{2,1,0:T(8,128)(2,1)S(1)}, bf16[32,48,896]{2,1,0:T(8,128)(2,1)}, u32[]{:S(2)}) copy-start(bf16[32,48,896]{2,1,0:T(8,128)(2,1)} %copy-done.6) | copy-start | bytes 8257540
  479.1 9.7 %all-to-all-start.4 = ((bf16[4,32,896]{2,1,0:T(8,128)(2,1)}), bf16[4,32,896]{2,1,0:T(8,128)(2,1)S(1)}, u32[]{:S(2)}, u32[]{:S(2)}) async-start(bf16[4,32,896]{2,1,0:T(8,128)(2,1)} %bitcast.25), calls=%async_computation.5 | async-start | bytes 458752 | tf_op jit(solution)/shard_map/all_to_all | solution.py:97
  488.8 14.3 %all-to-all-start.3 = ((bf16[4,32,896]{2,1,0:T(8,128)(2,1)}), bf16[4,32,896]{2,1,0:T(8,128)(2,1)S(1)}, u32[]{:S(2)}, u32[]{:S(2)}) async-start(bf16[4,32,896]{2,1,0:T(8,128)(2,1)} %bitcast.23), calls=%async_computation.4 | async-start | bytes 458752 | tf_op jit(solution)/shard_map/all_to_all | solution.py:96
  493.6 10.1 %copy-start.1 = (bf16[1,896,1024]{2,1,0:T(8,128)(2,1)S(1)}, bf16[1,896,1024]{2,1,0:T(8,128)(2,1)}, u32[]{:S(2)}) copy-start(bf16[1,896,1024]{2,1,0:T(8,128)(2,1)} %param.11) | copy-start | bytes 5505028
Sparse Core Ops, SparseCore 0:
  36.6 71.4 all-gather.4
  158.9 87.6 reduce-scatter.4
  250.9 92.8 all-gather.6
  476.1 15.6 reduce-scatter.6
where the time goes:
time: 521 us; the launch traced here: 511 us
  waiting for transfers between devices  317 us (61%)
  local copies, waits for them, and re-layouts  61.9 us (12%)
  matrix products  56.5 us (11%)
  starting transfers between devices  26.7 us (5%)
  other arithmetic  22.1 us (4%)
  between operations  14.4 us (3%)
  blocking collectives  11.9 us (2%)
    all_gather x1, waiting for transfers between devices, per_device(): terms = lax.all_gather(acts, 'dp', axis=0, tiled=False)  93 us
    reduce_scatter x1, waiting for transfers between devices, per_device(): pre = lax.psum_scatter(part, 'dp', scatter_dimension=0, tiled=True)  87.8 us
    all_gather x1, waiting for transfers between devices, dispatch(): lax.all_gather(jnp.concatenate([tok, grad, tab], axis=1), 'expert', axis=...  71.4 us
    all_to_all x1, waiting for transfers between devices, per_device(): lax.all_to_all(send, 'expert', split_axis=0, concat_axis=0, tiled=True)  61.9 us
    dot_general x11, matrix products, dot32(): return lax.dot_general(a, b, (dims, ((), ())), preferred_element_type=F32)  46.2 us
    unnamed x31, local copies, waits for them, and re-layouts  18.1 us
    reshape x1, local copies, waits for them, and re-layouts, per_device(): terms.reshape(n_dp, rows, 3, quarter).transpose(2, 1, 0, 3)  15.4 us
    all_gather x1, blocking collectives, dispatch(): tab = lax.all_gather(table, 'dp', axis=0, tiled=True)  11.9 us
  transfers between devices with their start and end apart: 9, of which 6 were waited for; matrix products, arithmetic and copies ran while one was open for 6% of the time, Pallas kernels for 0%

commit v1 on v0

--- a/solution.py
+++ b/solution.py
@@ -25,7 +25,9 @@
 
 def to_slices(array, n_dp):
     rows, width = array.shape
-    return lax.all_to_all(array, "dp", split_axis=1, concat_axis=0, tiled=True)
+    return jnp.concatenate(
+        lax.all_to_all(jnp.stack(jnp.split(array, lax.axis_size("dp"), axis=1)), "dp", 0, 0), axis=0
+    )
 
 
 def dispatch(tokens, out_grad, table):

time: 521 us -> 521 us (level)
  no operation moved by 1% of the time
where the time goes in v1:
time: 521 us; the launch traced here: 510 us
  waiting for transfers between devices  317 us (61%)
  local copies, waits for them, and re-layouts  62.4 us (12%)
  matrix products  54.7 us (10%)
  starting transfers between devices  26.7 us (5%)
  other arithmetic  23.3 us (4%)
  between operations  14.4 us (3%)
  blocking collectives  11.9 us (2%)
    all_gather x1, waiting for transfers between devices, per_device(): terms = lax.all_gather(acts, 'dp', axis=0, tiled=False)  93 us
    reduce_scatter x1, waiting for transfers between devices, per_device(): pre = lax.psum_scatter(part, 'dp', scatter_dimension=0, tiled=True)  87.8 us
    all_gather x1, waiting for transfers between devices, dispatch(): lax.all_gather(jnp.concatenate([tok, grad, tab], axis=1), 'expert', axis=...  71.4 us
    all_to_all x1, waiting for transfers between devices, per_device(): lax.all_to_all(send, 'expert', split_axis=0, concat_axis=0, tiled=True)  61.9 us
    dot_general x11, matrix products, dot32(): return lax.dot_general(a, b, (dims, ((), ())), preferred_element_type=F32)  44.4 us
    unnamed x31, local copies, waits for them, and re-layouts  18.1 us
    reshape x1, local copies, waits for them, and re-layouts, per_device(): terms.reshape(n_dp, rows, 3, quarter).transpose(2, 1, 0, 3)  15.4 us
    all_gather x1, blocking collectives, dispatch(): tab = lax.all_gather(table, 'dp', axis=0, tiled=True)  11.9 us
  transfers between devices with their start and end apart: 9, of which 6 were waited for; matrix products, arithmetic and copies ran while one was open for 6% of the time, Pallas kernels for 0%

profile of v1, /device:TPU:34, one launch (start us, length us, event | category | flops | bytes accessed | tf_op | source)
XLA Modules:
  0.0 510.5 jit_solution(3451805264861443530)
XLA Ops:
  7.2 1.1 slice_bitcast_fusion.3
  8.2 0.7 pad_maximum_fusion.5
  9.0 4.8 all-to-all-start.1
  13.8 0.8 copy.61
  14.7 0.9 slice_bitcast_fusion.7
  15.7 0.7 pad_maximum_fusion.4
  16.4 0.8 copy.62
  17.3 1.5 all-to-all-done.1
  18.8 4.8 all-to-all-start
  23.8 11.9 %all_gather.15 = bf16[128,128]{1,0:T(8,128)(2,1)S(1)} all-gather(bf16[32,128]{1,0:T(8,128)(2,1)S(1)} %pad_maximum_fusion.6), channel_id=1, replica_groups=mesh['dp'=4,'expert'=32] {'dp'}, dimensions={0}, use_global_device_ids=true | all-gather | bytes 40960 | tf_op jit(solution)/shard_map/all_gather | solution.py:37
  35.7 0.8 pad_maximum_fusion.3
  36.7 71.4 %all-gather.5.cloned.1.call-done = bf16[4096,1920]{1,0:T(8,128)(2,1)} async-done(((bf16[128,1920]{1,0:T(8,128)(2,1)}), bf16[4096,1920]{1,0:T(8,128)(2,1)}) %all-gather.5.cloned.1.call-update) | async-done | bytes 15728656 | tf_op jit(solution)/shard_map/all_gather | solution.py:38
  108.1 2.0 fusion.6
  110.1 6.4 %fusion = f32[32,48,1792]{2,1,0:T(8,128)S(1)} fusion(bf16[32,128,1920]{2,1,0:T(8,128)(2,1)} %bitcast.100, f32[32,128]{1,0:T(8,128)S(1)} %get-tuple-element.13, f32[48]{0:T(128)S(1)} %fusion.35, pred[48,128]{1,0:T(8,128)(4,1)S(1)} %broadcast_compare_fusion), kind=kOutput, calls=%fused_computation | convolution fusion | flops 705036288 | bytes 25712832 | tf_op jit(solution)/shard_map/dot_general | solution.py:53
  117.6 2.5 copy-done.9
  120.1 3.7 convolution_convert_fusion
  123.7 2.4 copy.67
  126.2 3.8 convolution_convert_fusion.2
  130.0 2.4 copy.65
  132.5 4.3 convolution_convert_fusion.1
  136.8 2.4 copy.66
  139.2 9.3 %pad_maximum_fusion = bf16[3,1536,4,256]{1,2,3,0:T(4,128)(2,1)} fusion(bf16[1,1536,4,256]{1,2,3,0:T(4,128)(2,1)S(1)} %copy.67, bf16[1,1536,4,256]{1,2,3,0:T(4,128)(2,1)S(1)} %copy.66, bf16[1,1536,4,256]{1,2,3,0:T(4,128)(2,1)S(1)} %copy.65), kind=kLoop, calls=%fused_computation.2 | loop fusion | flops 9437184 | bytes 18874368 | tf_op jit(solution)/shard_map/stack | solution.py:121
  148.5 10.4 %copy.80 = bf16[96,8,4,1536]{3,1,2,0:T(8,128)(2,1)} copy(bf16[96,8,4,1536]{3,2,1,0:T(4,128)(2,1)} %bitcast.103) | data formatting | bytes 18874368
  158.9 87.8 %reduce-scatter.5.cloned.1.call-done = bf16[1536,768]{0,1:T(8,128)(2,1)} async-done(((bf16[6144,768]{0,1:T(8,128)(2,1)}), bf16[1536,768]{0,1:T(8,128)(2,1)}) %reduce-scatter.5.cloned.1.call-update) | async-done | bytes 2359312 | tf_op jit(solution)/shard_map/reduce_scatter | solution.py:131
  246.7 2.6 fusion.14
  249.3 1.5 pad_maximum_fusion.2
  250.9 93.0 %all-gather.7.cloned.1.call-done = bf16[6144,768]{0,1:T(8,128)(2,1)} async-done(((bf16[1536,768]{0,1:T(8,128)(2,1)}), bf16[6144,768]{0,1:T(8,128)(2,1)}) %all-gather.7.cloned.1.call-update) | async-done | bytes 9437200 | tf_op jit(solution)/shard_map/all_gather | solution.py:133
  343.9 15.4 %reshape.278 = bf16[4,1536,3,256]{1,0,3,2:T(4,128)(2,1)} reshape(bf16[6144,768]{0,1:T(8,128)(2,1)} %all-gather.7.cloned.1.call-done) | data formatting | bytes 18874368 | tf_op jit(solution)/shard_map/reshape | solution.py:134
  359.3 6.1 %fusion.37 = (bf16[1,1536,4,256]{1,2,3,0:T(4,128)(2,1)S(1)}, bf16[1,1536,4,256]{1,2,3,0:T(4,128)(2,1)S(1)}, bf16[1,1536,4,256]{1,2,3,0:T(4,128)(2,1)S(1)}) fusion(bf16[3,1536,4,256]{1,2,3,0:T(4,128)(2,1)} %bitcast.102), kind=kLoop, calls=%fused_computation.99 | loop fusion | bytes 18874368 | tf_op jit(solution)/shard_map/slice | solution.py:135
  366.0 3.0 fusion.11
  370.2 2.3 copy-done.10
  372.5 3.3 convolution_convert_fusion.3
  375.9 3.3 add_convert_fusion
  379.1 2.8 pad_maximum_fusion.1
  381.9 7.9 %copy.71 = bf16[1536,1792]{1,0:T(8,128)(2,1)} copy(bf16[1536,1792]{0,1:T(8,128)(2,1)} %pad_maximum_fusion.1) | data formatting | bytes 11010048 | tf_op jit(solution)/shard_map/concatenate | solution.py:138
  389.8 7.5 %all-to-all-start.2 = ((bf16[32,48,1792]{2,1,0:T(8,128)(2,1)}), bf16[32,48,1792]{2,1,0:T(8,128)(2,1)}, u32[]{:S(2)}, u32[]{:S(2)}) async-start(bf16[32,48,1792]{2,1,0:T(8,128)(2,1)} %bitcast.104), calls=%async_computation.3 | async-start | bytes 11010048 | tf_op jit(solution)/shard_map/all_to_all | solution.py:139
  398.5 7.5 %convert_bitcast_fusion = bf16[1,1024,896]{2,1,0:T(8,128)(2,1)} fusion(bf16[1536,1024]{0,1:T(8,128)(2,1)} %bitcast.110, bf16[1536,896]{1,0:T(8,128)(2,1)} %bitcast.119), kind=kOutput, calls=%fused_computation.32 | convolution fusion | flops 2819489792 | bytes 7733248 | tf_op jit(solution)/shard_map/dot_general | solution.py:12
  406.0 4.4 convert_bitcast_fusion.1
  410.4 61.9 %all-to-all-done.2 = bf16[32,48,1792]{2,1,0:T(8,128)(2,1)} async-done(((bf16[32,48,1792]{2,1,0:T(8,128)(2,1)}), bf16[32,48,1792]{2,1,0:T(8,128)(2,1)}, u32[]{:S(2)}, u32[]{:S(2)}) %all-to-all-start.2) | async-done | bytes 5505056 | tf_op jit(solution)/shard_map/all_to_all | solution.py:139
  472.3 2.0 slice.82
  474.3 0.9 fusion.23
  475.9 3.1 fusion.24
  479.0 4.5 all-to-all-start.4
  483.6 4.0 convolution_convert_fusion.4
  487.5 1.2 all-to-all-done.4
  488.7 4.9 all-to-all-start.3
  493.6 7.1 %convert_bitcast_fusion.2 = bf16[1,896,1024]{2,1,0:T(8,128)(2,1)} fusion(bf16[1536,896]{1,0:T(8,128)(2,1)} %bitcast.116, bf16[1536,1024]{0,1:T(8,128)(2,1)} %bitcast.106), kind=kOutput, calls=%fused_computation.34 | convolution fusion | flops 2819489792 | bytes 7733248 | tf_op jit(solution)/shard_map/dot_general | solution.py:12
  500.7 0.9 select_reduce_fusion.1
  (66 shorter events, 7.3 us)
Async XLA Ops:
  7.2 119.0 %copy-start = (bf16[1,896,1024]{2,1,0:T(8,128)(2,1)S(1)}, bf16[1,896,1024]{2,1,0:T(8,128)(2,1)}, u32[]{:S(2)}) copy-start(bf16[1,896,1024]{2,1,0:T(8,128)(2,1)} %param.11) | copy-start | bytes 5505028
  9.0 9.9 %all-to-all-start.1 = ((bf16[4,32,896]{2,1,0:T(8,128)(2,1)}), bf16[4,32,896]{2,1,0:T(8,128)(2,1)S(1)}, u32[]{:S(2)}, u32[]{:S(2)}) async-start(bf16[4,32,896]{2,1,0:T(8,128)(2,1)} %pad_maximum_fusion.5), calls=%async_computation.1 | async-start | bytes 458752 | tf_op jit(solution)/shard_map/all_to_all | solution.py:29
  18.8 16.8 %all-to-all-start = ((bf16[4,32,896]{2,1,0:T(8,128)(2,1)}), bf16[4,32,896]{2,1,0:T(8,128)(2,1)S(1)}, u32[]{:S(2)}, u32[]{:S(2)}) async-start(bf16[4,32,896]{2,1,0:T(8,128)(2,1)} %pad_maximum_fusion.4), calls=%async_computation | async-start | bytes 458752 | tf_op jit(solution)/shard_map/all_to_all | solution.py:29
  23.7 84.5 %all-gather.5.cloned.1.call-start = ((), (), s32[]{:S(2)}) async-start(), calls=%async_computation.8 | async-start | bytes 16220160 | tf_op jit(solution)/shard_map/all_gather | solution.py:38
  36.5 210.2 %reduce-scatter.5.cloned.1.call-start = ((), (), s32[]{:S(2)}) async-start(), calls=%async_computation.7 | async-start | bytes 11796480 | tf_op jit(solution)/shard_map/reduce_scatter | solution.py:131
  117.2 15.3 %copy-start.6 = (bf16[32,48,896]{2,1,0:T(8,128)(2,1)}, bf16[32,48,896]{2,1,0:T(8,128)(2,1)S(1)}, u32[]{:S(2)}) copy-start(bf16[32,48,896]{2,1,0:T(8,128)(2,1)S(1)} %slice.113) | copy-start | bytes 8257540
  117.2 2.9 copy-start.9
  117.6 6.2 %copy-start.8 = (bf16[32,48,896]{2,1,0:T(8,128)(2,1)}, bf16[32,48,896]{2,1,0:T(8,128)(2,1)S(1)}, u32[]{:S(2)}) copy-start(bf16[32,48,896]{2,1,0:T(8,128)(2,1)S(1)} %fusion.2) | copy-start | bytes 8257540
  130.0 2.5 copy-start.11
  158.8 185.1 %all-gather.7.cloned.1.call-start = ((), (), s32[]{:S(2)}) async-start(), calls=%async_computation.9 | async-start | bytes 11796480 | tf_op jit(solution)/shard_map/all_gather | solution.py:133
  366.0 3.0 copy-start.2
  369.6 6.3 %copy-start.3 = (bf16[1,1536,4,256]{1,3,2,0:T(8,128)(2,1)}, bf16[1,1536,4,256]{1,3,2,0:T(8,128)(2,1)S(1)}, u32[]{:S(2)}) copy-start(bf16[1,1536,4,256]{1,3,2,0:T(8,128)(2,1)S(1)} %copy.70) | copy-start | bytes 9437188
  369.6 2.9 copy-start.10
  370.2 5.6 %copy-start.5 = (bf16[1,1536,4,256]{1,3,2,0:T(8,128)(2,1)}, bf16[1,1536,4,256]{1,3,2,0:T(8,128)(2,1)S(1)}, u32[]{:S(2)}) copy-start(bf16[1,1536,4,256]{1,3,2,0:T(8,128)(2,1)S(1)} %copy.68) | copy-start | bytes 9437188
  372.5 3.4 copy-start.12
  389.8 82.4 %all-to-all-start.2 = ((bf16[32,48,1792]{2,1,0:T(8,128)(2,1)}), bf16[32,48,1792]{2,1,0:T(8,128)(2,1)}, u32[]{:S(2)}, u32[]{:S(2)}) async-start(bf16[32,48,1792]{2,1,0:T(8,128)(2,1)} %bitcast.104), calls=%async_computation.3 | async-start | bytes 11010048 | tf_op jit(solution)/shard_map/all_to_all | solution.py:139
  397.4 103.3 %reduce-scatter.7.cloned.1.call-start = ((), (), s32[]{:S(2)}) async-start(), calls=%async_computation.10 | async-start | bytes 81920 | tf_op jit(solution)/shard_map/reduce_scatter | solution.py:100
  398.5 7.5 %copy-start.4 = (bf16[1,1536,4,256]{1,3,2,0:T(8,128)(2,1)S(1)}, bf16[1,1536,4,256]{1,3,2,0:T(8,128)(2,1)}, u32[]{:S(2)}) copy-start(bf16[1,1536,4,256]{1,3,2,0:T(8,128)(2,1)} %copy-done.3) | copy-start | bytes 9437188
  398.5 7.5 %copy-start.7 = (bf16[32,48,896]{2,1,0:T(8,128)(2,1)S(1)}, bf16[32,48,896]{2,1,0:T(8,128)(2,1)}, u32[]{:S(2)}) copy-start(bf16[32,48,896]{2,1,0:T(8,128)(2,1)} %copy-done.6) | copy-start | bytes 8257540
  479.0 9.7 %all-to-all-start.4 = ((bf16[4,32,896]{2,1,0:T(8,128)(2,1)}), bf16[4,32,896]{2,1,0:T(8,128)(2,1)S(1)}, u32[]{:S(2)}, u32[]{:S(2)}) async-start(bf16[4,32,896]{2,1,0:T(8,128)(2,1)} %bitcast.31), calls=%async_computation.5 | async-start | bytes 458752 | tf_op jit(solution)/shard_map/all_to_all | solution.py:99
  488.7 14.3 %all-to-all-start.3 = ((bf16[4,32,896]{2,1,0:T(8,128)(2,1)}), bf16[4,32,896]{2,1,0:T(8,128)(2,1)S(1)}, u32[]{:S(2)}, u32[]{:S(2)}) async-start(bf16[4,32,896]{2,1,0:T(8,128)(2,1)} %bitcast.29), calls=%async_computation.4 | async-start | bytes 458752 | tf_op jit(solution)/shard_map/all_to_all | solution.py:98
  493.6 10.1 %copy-start.1 = (bf16[1,896,1024]{2,1,0:T(8,128)(2,1)S(1)}, bf16[1,896,1024]{2,1,0:T(8,128)(2,1)}, u32[]{:S(2)}) copy-start(bf16[1,896,1024]{2,1,0:T(8,128)(2,1)} %param.11) | copy-start | bytes 5505028
Sparse Core Ops, SparseCore 0:
  36.6 71.4 all-gather.4
  159.0 87.7 reduce-scatter.4
  251.0 92.8 all-gather.6
  476.1 15.6 reduce-scatter.6
